TPU v7x, 512 devices: a whole 4x8x8 slice. The times are simulated.
512 devices in a mesh: dp: 64 (over y, x, core), mp: 8 (over z).
Axes of the slice: x: 4, y: 8, z: 8, core: 2. Of those that a mesh axis runs over, the one named last changes fastest.
Arguments:
- tokens: bfloat16 [32768, 2048], P('dp'), may hold values from -6 to 6
- q_weight: bfloat16 [2048, 256], P('dp', 'mp'), may hold values from -0.125 to 0.125
- k_weight: bfloat16 [2048, 256], P('dp', 'mp'), may hold values from -0.125 to 0.125
- v_weight: bfloat16 [2048, 2048], P('dp', 'mp'), may hold values from -0.125 to 0.125
- adapter_down: bfloat16 [2048, 256], P(None, 'mp'), may hold values from -0.125 to 0.125
- adapter_up: bfloat16 [256, 2048], P(None, 'mp'), may hold values from -1.5 to 1.5
- lengths: int32 [4], replicated, may hold values from 1 to 16384, 32768 in all
- adapter_ids: int32 [4], replicated, may hold values from 0 to 15
- head_gain: float32 [2048], P('mp'), may hold values from 0.1 to 1.9
- out_weight: bfloat16 [2048, 2048], P('mp', 'dp'), may hold values from -0.125 to 0.125
Outputs:
- layer_out: bfloat16 [32768, 2048], P('dp', 'mp')
Inputs may be any that keep to these rules, and one draw needn't show every extreme that they name: The lengths sum to 32768 and the longest request has exactly 32768 // 2 tokens.
All inputs are finite; a program needn't handle non-finite values.
Results may differ from a plain program's by a relative error of at most 0.022.
Values may be sent and summed in bfloat16 or wider, within the bound.
A program may use at most 128 MiB of HBM per device.

v0:
```python
import math
import jax
import jax.numpy as jnp
from jax import lax
from jax.sharding import PartitionSpec as P

F = 16
R = 16
EPSILON = 1e-05


def carried_in(value, axis, combine, identity):
    length, place = (lax.axis_size(axis), lax.axis_index(axis))
    everything = jax.tree.map(
        lambda part, kind: lax.all_gather(part.astype(kind), axis),
        value,
        (jnp.bfloat16, jnp.bfloat16),
    )
    start = jax.tree.map(
        lambda part, zero: jnp.broadcast_to(jnp.asarray(zero, part.dtype), part.shape),
        value,
        identity,
    )

    def turn(k, before):
        reached = k < place
        new = combine(
            before, jax.tree.map(lambda part, own: part[k].astype(own.dtype), everything, value)
        )
        return jax.tree.map(lambda a, b: jnp.where(reached, a, b), new, before)

    return lax.fori_loop(0, length, turn, start)


def taylor(inputs):
    squares = (inputs[..., :, None] * inputs[..., None, :]).reshape(
        inputs.shape[:-1] + (inputs.shape[-1] * inputs.shape[-1],)
    )
    constant = jnp.ones(inputs.shape[:-1] + (1,), jnp.float32)
    return jnp.concatenate([constant, 0.5 * inputs, squares * (0.25 / math.sqrt(2.0))], axis=-1)


def token_tables(lengths, adapter_ids, positions):
    bounds = jnp.cumsum(lengths)
    request = jnp.sum((positions[:, None] >= bounds[None, :]).astype(jnp.int32), axis=1)
    openings = bounds - lengths
    starts = jnp.any(positions[:, None] == openings[None, :], axis=1)
    picked = request[:, None] == jnp.arange(lengths.shape[0], dtype=jnp.int32)[None, :]
    adapter = jnp.sum(jnp.where(picked, adapter_ids[None, :], 0), axis=1)
    return (request, starts, adapter)


def block_local(query, key_rows, values, request, starts):
    scores = jnp.einsum("ihd,jhd->hij", query, key_rows, preferred_element_type=jnp.float32) * 0.25
    weights = 1.0 + scores + 0.5 * scores * scores
    indexes = jnp.arange(request.shape[0], dtype=jnp.int32)
    allowed = (indexes[None, :] <= indexes[:, None]) & (request[None, :] == request[:, None])
    weights = jnp.where(allowed[None], weights, 0.0).astype(jnp.bfloat16)
    within = jnp.einsum("hij,jhe->ihe", weights, values, preferred_element_type=jnp.float32)
    query_map = taylor(query.astype(jnp.float32)).astype(jnp.bfloat16)
    key_map = taylor(key_rows.astype(jnp.float32)).astype(jnp.bfloat16)
    tail_mask = (request == request[-1]).astype(jnp.bfloat16)
    masked_keys = key_map * tail_mask[:, None, None]
    summary = jnp.einsum("ihf,ihe->hfe", masked_keys, values, preferred_element_type=jnp.float32)
    restart = jnp.max(starts.astype(jnp.float32))
    return (within, query_map, summary, restart)


def finish(within, query_map, carried, request, starts, gains):
    follows = ((request == request[0]) & jnp.logical_not(starts[0])).astype(jnp.float32)
    cross = jnp.einsum(
        "ihf,hfe->ihe", query_map, carried.astype(jnp.bfloat16), preferred_element_type=jnp.float32
    )
    combined = within + follows[:, None, None] * cross
    factor = lax.rsqrt(jnp.mean(combined * combined, axis=-1, keepdims=True) + EPSILON)
    return (combined * factor * gains[None]).astype(jnp.bfloat16)


def combine(earlier, later):
    return (
        jnp.maximum(earlier[0], later[0]),
        jnp.where(later[0] > 0, later[1], earlier[1] + later[1]),
    )


def per_device(
    tokens,
    q_weight,
    k_weight,
    v_weight,
    adapter_down,
    adapter_up,
    lengths,
    adapter_ids,
    head_gain,
    out_weight,
):
    row_count = tokens.shape[0]
    heads_here = q_weight.shape[1] // F
    value_width = v_weight.shape[1] // heads_here
    positions = lax.axis_index("dp") * row_count + jnp.arange(row_count, dtype=jnp.int32)
    request, starts, adapter = token_tables(lengths, adapter_ids, positions)
    query_sum = jnp.dot(
        tokens,
        lax.all_gather(q_weight, "dp", axis=0, tiled=True),
        preferred_element_type=jnp.float32,
    )
    key_sum = jnp.dot(
        tokens,
        lax.all_gather(k_weight, "dp", axis=0, tiled=True),
        preferred_element_type=jnp.float32,
    )
    value_sum = jnp.dot(
        tokens,
        lax.all_gather(v_weight, "dp", axis=0, tiled=True),
        preferred_element_type=jnp.float32,
    )
    query = query_sum.astype(jnp.bfloat16).reshape(row_count, heads_here, F)
    key_rows = key_sum.astype(jnp.bfloat16).reshape(row_count, heads_here, F)
    piece = lax.all_gather(adapter_down, "mp", axis=1, tiled=True)
    partial_low = jnp.dot(tokens, piece, preferred_element_type=jnp.float32)
    owners = jnp.arange(piece.shape[1], dtype=jnp.int32) // R
    low_rank = jnp.where(adapter[:, None] == owners[None, :], partial_low, 0.0).astype(jnp.bfloat16)
    values = value_sum + jnp.dot(low_rank, adapter_up, preferred_element_type=jnp.float32)
    values = values.astype(jnp.bfloat16).reshape(row_count, heads_here, value_width)
    within, query_map, summary, restart = block_local(query, key_rows, values, request, starts)
    identity = (jnp.zeros((), jnp.float32), jnp.zeros_like(summary))
    _, carried = carried_in((restart, summary), "dp", combine, identity)
    gains = head_gain.reshape(heads_here, value_width)
    normed = finish(within, query_map, carried, request, starts, gains).reshape(
        row_count, heads_here * value_width
    )
    partial_terms = jnp.dot(
        normed,
        lax.all_gather(out_weight, "dp", axis=1, tiled=True),
        preferred_element_type=jnp.float32,
    )
    return lax.psum_scatter(
        partial_terms.astype(jnp.bfloat16), "mp", scatter_dimension=1, tiled=True
    )


def solution(mesh):
    placed = (
        P("dp", None),
        P("dp", "mp"),
        P("dp", "mp"),
        P("dp", "mp"),
        P(None, "mp"),
        P(None, "mp"),
        P(),
        P(),
        P("mp"),
        P("mp", "dp"),
    )
    return jax.shard_map(
        per_device, mesh=mesh, in_specs=placed, out_specs=P("dp", "mp"), check_vma=False
    )
```

profile of v0, /device:TPU:6, one launch (start us, length us, event | category | flops | bytes accessed | tf_op | source)
XLA Modules:
  0.0 530.6 jit_solution(14623870171346762429)
XLA Ops:
  9.7 52.8 %all_gather.30 = bf16[2048,32]{1,0:T(8,128)(2,1)S(1)} all-gather(bf16[32,32]{1,0:T(8,128)(2,1)} %param.14), channel_id=1, replica_groups=mesh['dp'=64,'mp'=8] {'dp'}, dimensions={0}, use_global_device_ids=true | all-gather | bytes 133120 | tf_op jit(solution)/shard_map/all_gather | solution.py:110
  64.0 1.3 compare_convert_fusion
  65.5 2.2 fusion.6
  67.7 70.5 %all-gather.6.cloned.1.call-done = bf16[2048,256]{1,0:T(8,128)(2,1)} async-done(((bf16[32,256]{1,0:T(8,128)(2,1)}), bf16[2048,256]{1,0:T(8,128)(2,1)}) %all-gather.6.cloned.1.call-update) | async-done | bytes 1048592 | tf_op jit(solution)/shard_map/all_gather | solution.py:115
  138.2 2.0 fusion.4
  140.9 1.1 convolution_convert_fusion.1
  143.5 48.5 %all_gather.29 = bf16[2048,32]{1,0:T(8,128)(2,1)S(1)} all-gather(bf16[32,32]{1,0:T(8,128)(2,1)S(1)} %copy-done.1), channel_id=1, replica_groups=mesh['dp'=64,'mp'=8] {'dp'}, dimensions={0}, use_global_device_ids=true | all-gather | bytes 133120 | tf_op jit(solution)/shard_map/all_gather | solution.py:105
  192.8 1.3 dynamic-slice
  194.1 1.4 dynamic-update-slice
  195.6 113.9 %all-reduce = bf16[64]{0:T(256)(128)(2,1)S(1)} all-reduce(bf16[64]{0:T(256)(128)(2,1)S(1)} %dynamic-update-slice), channel_id=1, replica_groups=mesh['dp'=64,'mp'=8] {'dp'}, use_global_device_ids=true, to_apply=%add | all-reduce | flops 64 | bytes 256
  309.5 2.8 fusion.1
  312.3 149.2 %while.14 = (s32[]{:T(128)}, f32[2,273,128]{2,1,0:T(8,128)S(1)}, s32[]{:T(128)}, bf16[64]{0:T(256)(128)(2,1)S(1)}, bf16[64,2,273,128]{3,2,1,0:T(8,128)(2,1)}, /*index=5*/s32[]{:T(128)}, s32[]{:T(128)}, f32[1]{0:T(128)}) while((s32[]{:T(128)}, f32[2,273,128]{2,1,0:T(8,128)S(1)}, s32[]{:T(128)}, bf16[64]{0:T(256)(128)(2,1)S(1)}, ...), condition=%wide.region_6.7_spmd.clone, body=%wide.region_5.6_spmd.clone.sunk | while | flops 349445 | bytes 699005 | solution.py:32
  315.9 1.1 fusion.52
  318.2 1.1 fusion.52
  320.6 1.1 fusion.52
  322.9 1.1 fusion.52
  325.2 1.1 fusion.52
  327.5 1.1 fusion.52
  329.9 1.1 fusion.52
  332.2 1.1 fusion.52
  334.5 1.1 fusion.52
  461.6 1.5 multiply_reduce_fusion
  463.3 3.3 convolution_convert_fusion
  466.6 57.5 %reduce-scatter.2.cloned.1.call-done = bf16[512,256]{1,0:T(8,128)(2,1)} async-done(((bf16[512,2048]{1,0:T(8,128)(2,1)}), bf16[512,256]{1,0:T(8,128)(2,1)}) %reduce-scatter.2.cloned.1.call-update) | async-done | bytes 262160 | tf_op jit(solution)/shard_map/reduce_scatter | solution.py:138
  (167 shorter events, 104.0 us)
Async XLA Ops:
  6.5 56.0 %copy-start = (bf16[512,2048]{1,0:T(8,128)(2,1)S(1)}, bf16[512,2048]{1,0:T(8,128)(2,1)}, u32[]{:S(2)}) copy-start(bf16[512,2048]{1,0:T(8,128)(2,1)} %param.12) | copy-start | bytes 6291460
  6.5 57.4 %copy-start.3 = (s32[4]{0:T(128)S(1)}, s32[4]{0:T(128)}, u32[]{:S(2)}) copy-start(s32[4]{0:T(128)} %param.19) | copy-start | bytes 52
  6.5 58.9 %copy-start.4 = (bf16[256,256]{1,0:T(8,128)(2,1)S(1)}, bf16[256,256]{1,0:T(8,128)(2,1)}, u32[]{:S(2)}) copy-start(bf16[256,256]{1,0:T(8,128)(2,1)} %param.17) | copy-start | bytes 393220
  6.5 58.9 %all-gather.8.cloned.1.call-start = ((), (), s32[]{:S(2)}) async-start(), calls=%async_computation.2 | async-start | bytes 1179648 | tf_op jit(solution)/shard_map/all_gather | solution.py:120
  7.3 130.9 %all-gather.6.cloned.1.call-start = ((), (), s32[]{:S(2)}) async-start(), calls=%async_computation.1 | async-start | bytes 1064960 | tf_op jit(solution)/shard_map/all_gather | solution.py:115
  8.0 304.3 %all-gather.12.cloned.1.call-start = ((), (), s32[]{:S(2)}) async-start(), calls=%async_computation.5 | async-start | bytes 9318400 | tf_op jit(solution)/shard_map/all_gather | solution.py:15
  140.2 0.7 copy-start.5
  140.2 3.3 copy-start.1
  142.0 321.2 %all-gather.10.cloned.1.call-start = ((), (), s32[]{:S(2)}) async-start(), calls=%async_computation.3 | async-start | bytes 1064960 | tf_op jit(solution)/shard_map/all_gather | solution.py:135
  142.6 381.5 %reduce-scatter.2.cloned.1.call-start = ((), (), s32[]{:S(2)}) async-start(), calls=%async_computation.4 | async-start | bytes 2359296 | tf_op jit(solution)/shard_map/reduce_scatter | solution.py:138
  312.3 150.8 %copy-start.2 = (f32[256]{0:T(256)S(1)}, f32[256]{0:T(256)}, u32[]{:S(2)}) copy-start(f32[256]{0:T(256)} %param.20) | copy-start | bytes 3076
Sparse Core Ops, SparseCore 0:
  9.4 46.9 all-gather.7
  59.7 78.4 all-gather.5
  142.1 86.8 all-gather.11
  232.3 80.0 all-gather.9
  466.7 57.2 reduce-scatter.1
where the time goes:
time: 533 us; the launch traced here: 531 us
  blocking collectives  215 us (40%)
  waiting for transfers between devices  130 us (24%)
  other arithmetic  72.4 us (14%)
  loops' own time  43.5 us (8%)
  local copies, waits for them, and re-layouts  41.7 us (8%)
  matrix products  14.4 us (3%)
  between operations  13.4 us (3%)
    unnamed x1, blocking collectives  114 us
    all_gather x1, waiting for transfers between devices, per_device(): lax.all_gather(v_weight, 'dp', axis=0, tiled=True)  70.5 us
    select_n x64, other arithmetic, turn(): return jax.tree.map(lambda a, b: jnp.where(reached, a, b), new, before)  68.1 us
    reduce_scatter x1, waiting for transfers between devices, per_device(): lax.psum_scatter(partial_terms.astype(jnp.bfloat16), 'mp', scatter_dimens...  57.5 us
    all_gather x1, blocking collectives, per_device(): lax.all_gather(k_weight, 'dp', axis=0, tiled=True)  52.8 us
    all_gather x1, blocking collectives, per_device(): lax.all_gather(q_weight, 'dp', axis=0, tiled=True)  48.5 us
    another operation x1, loops' own time, carried_in(): return lax.fori_loop(0, length, turn, start)  43.5 us
    dynamic_slice x64, local copies, waits for them, and re-layouts, turn(): part[k].astype(own.dtype)  37.6 us
  transfers between devices with their start and end apart: 5, of which 2 were waited for; matrix products, arithmetic and copies ran while one was open for 23% of the time, Pallas kernels for 0%

commit v1 on v0

--- a/solution.py
+++ b/solution.py
@@ -112,7 +112,9 @@
     )
     value_sum = jnp.dot(
         tokens,
-        lax.all_gather(v_weight, "dp", axis=0, tiled=True),
+        jnp.concatenate(
+            lax.all_to_all(jnp.stack([v_weight] * lax.axis_size("dp")), "dp", 0, 0), axis=0
+        ),
         preferred_element_type=jnp.float32,
     )
     query = query_sum.astype(jnp.bfloat16).reshape(row_count, heads_here, F)

time: 533 us -> 492 us (0.923)
  waiting for transfers between devices: 130 us -> 63.1 us
  blocking collectives: 215 us -> 230 us
  starting transfers between devices: 0.16 us -> 10.7 us
    all_gather x1 -> x0, waiting for transfers between devices: 70.5 us -> none  [per_device(): lax.all_gather(v_weight, 'dp', axis=0, tiled=True)]
    all_gather x1, blocking collectives: 52.8 us -> 67.7 us  [per_device(): lax.all_gather(k_weight, 'dp', axis=0, tiled=True)]
    all_to_all x0 -> x1, starting transfers between devices: none -> 10.6 us  [per_device(): lax.all_to_all(jnp.stack([v_weight] * lax.axis_size('dp')), 'dp', 0, 0)]
  transfers between devices with their start and end apart: 5 -> 5, of which waited for: 2 -> 1; matrix products, arithmetic and copies ran while one was open for 23% -> 25% of each run, Pallas kernels for 0% -> 0%
where the time goes in v1:
time: 492 us; the launch traced here: 490 us
  blocking collectives  230 us (47%)
  other arithmetic  71.9 us (15%)
  waiting for transfers between devices  63.1 us (13%)
  loops' own time  43.5 us (9%)
  local copies, waits for them, and re-layouts  43.3 us (9%)
  matrix products  14 us (3%)
  between operations  13.4 us (3%)
  starting transfers between devices  10.7 us (2%)
    unnamed x1, blocking collectives  115 us
    select_n x64, other arithmetic, turn(): return jax.tree.map(lambda a, b: jnp.where(reached, a, b), new, before)  68.1 us
    all_gather x1, blocking collectives, per_device(): lax.all_gather(k_weight, 'dp', axis=0, tiled=True)  67.7 us
    reduce_scatter x1, waiting for transfers between devices, per_device(): lax.psum_scatter(partial_terms.astype(jnp.bfloat16), 'mp', scatter_dimens...  61.7 us
    all_gather x1, blocking collectives, per_device(): lax.all_gather(q_weight, 'dp', axis=0, tiled=True)  47.8 us
    another operation x1, loops' own time, carried_in(): return lax.fori_loop(0, length, turn, start)  43.5 us
    dynamic_slice x64, local copies, waits for them, and re-layouts, turn(): part[k].astype(own.dtype)  37.6 us
    all_to_all x1, starting transfers between devices, per_device(): lax.all_to_all(jnp.stack([v_weight] * lax.axis_size('dp')), 'dp', 0, 0)  10.6 us
  transfers between devices with their start and end apart: 5, of which 1 were waited for; matrix products, arithmetic and copies ran while one was open for 25% of the time, Pallas kernels for 0%

profile of v1, /device:TPU:6, one launch (start us, length us, event | category | flops | bytes accessed | tf_op | source)
XLA Modules:
  0.0 490.1 jit_solution(12692136405493997413)
XLA Ops:
  7.3 1.9 stack.2
  9.1 10.6 %all-to-all-start = ((bf16[64,32,256]{2,1,0:T(8,128)(2,1)}), bf16[64,32,256]{2,1,0:T(8,128)(2,1)S(1)}, u32[]{:S(2)}, u32[]{:S(2)}) async-start(bf16[64,32,256]{2,1,0:T(8,128)(2,1)} %stack.2), calls=%async_computation | async-start | bytes 2097152 | tf_op jit(solution)/shard_map/all_to_all | solution.py:116
  20.1 67.7 %all_gather.26 = bf16[2048,32]{1,0:T(8,128)(2,1)S(1)} all-gather(bf16[32,32]{1,0:T(8,128)(2,1)S(1)} %copy-done.2), channel_id=1, replica_groups=mesh['dp'=64,'mp'=8] {'dp'}, dimensions={0}, use_global_device_ids=true | all-gather | bytes 133120 | tf_op jit(solution)/shard_map/all_gather | solution.py:110
  89.4 1.3 compare_convert_fusion
  91.6 3.0 fusion.6
  94.6 1.9 fusion.4
  97.2 1.1 convolution_convert_fusion.1
  100.0 47.8 %all_gather.25 = bf16[2048,32]{1,0:T(8,128)(2,1)S(1)} all-gather(bf16[32,32]{1,0:T(8,128)(2,1)S(1)} %copy-done.3), channel_id=1, replica_groups=mesh['dp'=64,'mp'=8] {'dp'}, dimensions={0}, use_global_device_ids=true | all-gather | bytes 133120 | tf_op jit(solution)/shard_map/all_gather | solution.py:105
  148.6 1.2 dynamic-slice
  149.8 1.3 dynamic-update-slice
  151.1 114.6 %all-reduce = bf16[64]{0:T(256)(128)(2,1)S(1)} all-reduce(bf16[64]{0:T(256)(128)(2,1)S(1)} %dynamic-update-slice), channel_id=1, replica_groups=mesh['dp'=64,'mp'=8] {'dp'}, use_global_device_ids=true, to_apply=%add | all-reduce | flops 64 | bytes 256
  265.8 2.8 fusion.1
  268.6 149.2 %while.14 = (s32[]{:T(128)}, f32[2,273,128]{2,1,0:T(8,128)S(1)}, s32[]{:T(128)}, bf16[64]{0:T(256)(128)(2,1)S(1)}, bf16[64,2,273,128]{3,2,1,0:T(8,128)(2,1)}, /*index=5*/s32[]{:T(128)}, s32[]{:T(128)}, f32[1]{0:T(128)}) while((s32[]{:T(128)}, f32[2,273,128]{2,1,0:T(8,128)S(1)}, s32[]{:T(128)}, bf16[64]{0:T(256)(128)(2,1)S(1)}, ...), condition=%wide.region_6.7_spmd.clone, body=%wide.region_5.6_spmd.clone.sunk | while | flops 349445 | bytes 699005 | solution.py:32
  272.2 1.1 fusion.52
  274.5 1.1 fusion.52
  276.8 1.1 fusion.52
  279.2 1.1 fusion.52
  281.5 1.1 fusion.52
  283.8 1.1 fusion.52
  286.2 1.1 fusion.52
  288.5 1.1 fusion.52
  290.8 1.1 fusion.52
  418.5 3.3 convolution_convert_fusion
  421.9 61.7 %reduce-scatter.2.cloned.1.call-done = bf16[512,256]{1,0:T(8,128)(2,1)} async-done(((bf16[512,2048]{1,0:T(8,128)(2,1)}), bf16[512,256]{1,0:T(8,128)(2,1)}) %reduce-scatter.2.cloned.1.call-update) | async-done | bytes 262160 | tf_op jit(solution)/shard_map/reduce_scatter | solution.py:140
  (175 shorter events, 103.4 us)
Async XLA Ops:
  6.5 81.3 %copy-start = (bf16[512,2048]{1,0:T(8,128)(2,1)S(1)}, bf16[512,2048]{1,0:T(8,128)(2,1)}, u32[]{:S(2)}) copy-start(bf16[512,2048]{1,0:T(8,128)(2,1)} %param.12) | copy-start | bytes 6291460
  6.5 13.3 %copy-start.7 = (s32[4]{0:T(128)S(1)}, s32[4]{0:T(128)}, u32[]{:S(2)}) copy-start(s32[4]{0:T(128)} %param.18) | copy-start | bytes 52
  6.5 13.6 %copy-start.2 = (bf16[32,32]{1,0:T(8,128)(2,1)S(1)}, bf16[32,32]{1,0:T(8,128)(2,1)}, u32[]{:S(2)}) copy-start(bf16[32,32]{1,0:T(8,128)(2,1)} %param.14) | copy-start | bytes 6148
  6.5 85.1 %all-gather.5.cloned.1.call-start = ((), (), s32[]{:S(2)}) async-start(), calls=%async_computation.2 | async-start | bytes 1179648 | tf_op jit(solution)/shard_map/all_gather | solution.py:122
  9.1 85.5 %all-to-all-start = ((bf16[64,32,256]{2,1,0:T(8,128)(2,1)}), bf16[64,32,256]{2,1,0:T(8,128)(2,1)S(1)}, u32[]{:S(2)}, u32[]{:S(2)}) async-start(bf16[64,32,256]{2,1,0:T(8,128)(2,1)} %stack.2), calls=%async_computation | async-start | bytes 2097152 | tf_op jit(solution)/shard_map/all_to_all | solution.py:116
  19.7 69.6 %copy-start.5 = (s32[4]{0:T(128)S(1)}, s32[4]{0:T(128)}, u32[]{:S(2)}) copy-start(s32[4]{0:T(128)} %param.19) | copy-start | bytes 52
  19.7 71.9 %copy-start.6 = (bf16[256,256]{1,0:T(8,128)(2,1)S(1)}, bf16[256,256]{1,0:T(8,128)(2,1)}, u32[]{:S(2)}) copy-start(bf16[256,256]{1,0:T(8,128)(2,1)} %param.17) | copy-start | bytes 393220
  19.7 248.8 %all-gather.9.cloned.1.call-start = ((), (), s32[]{:S(2)}) async-start(), calls=%async_computation.5 | async-start | bytes 9318400 | tf_op jit(solution)/shard_map/all_gather | solution.py:15
  94.6 2.6 copy-start.1
  96.5 0.7 copy-start.8
  96.5 3.5 copy-start.3
  98.4 320.1 %all-gather.7.cloned.1.call-start = ((), (), s32[]{:S(2)}) async-start(), calls=%async_computation.3 | async-start | bytes 1064960 | tf_op jit(solution)/shard_map/all_gather | solution.py:137
  99.1 384.4 %reduce-scatter.2.cloned.1.call-start = ((), (), s32[]{:S(2)}) async-start(), calls=%async_computation.4 | async-start | bytes 2359296 | tf_op jit(solution)/shard_map/reduce_scatter | solution.py:140
  268.6 149.3 %copy-start.9 = (f32[2,128,512]{2,1,0:T(8,128)S(1)}, f32[2,128,512]{2,1,0:T(8,128)}, u32[]{:S(2)}) copy-start(f32[2,128,512]{2,1,0:T(8,128)} %fusion.1) | copy-start | bytes 1572868
  268.6 149.8 %copy-start.4 = (f32[256]{0:T(256)S(1)}, f32[256]{0:T(256)}, u32[]{:S(2)}) copy-start(f32[256]{0:T(256)} %param.20) | copy-start | bytes 3076
Sparse Core Ops, SparseCore 0:
  9.4 46.7 all-gather.4
  98.5 91.2 all-gather.8
  193.1 79.8 all-gather.6
  422.0 61.5 reduce-scatter.1
